TPU v7x, 256 devices: a whole 4x4x8 slice. The times are simulated.
256 devices in a mesh: dp: 8 (over y, core), ctx: 32 (over x, z).
Axes of the slice: x: 4, y: 4, z: 8, core: 2. Of those that a mesh axis runs over, the one named last changes fastest.
Arguments:
- query_rows: bfloat16 [8, 16384, 1024], P('dp', 'ctx'), may hold values from -6 to 6
- key_rows: bfloat16 [8, 16384, 1024], P('dp', 'ctx'), may hold values from -6 to 6
- value_rows: bfloat16 [8, 16384, 1024], P('dp', 'ctx'), may hold values from -6 to 6
- query_gain: float32 [128], replicated, may hold values from 0.5 to 1.5
- key_gain: float32 [128], replicated, may hold values from 0.5 to 1.5
- selected: int32 [8, 32, 3], P('dp', 'ctx'), may hold values from 0 to 30, as said below
- output_grad: bfloat16 [8, 16384, 1024], P('dp', 'ctx'), may hold values from -6 to 6
Outputs:
- attended: bfloat16 [8, 16384, 1024], P('dp', 'ctx')
- query_grad: bfloat16 [8, 16384, 1024], P('dp', 'ctx')
- key_grad: bfloat16 [8, 16384, 1024], P('dp', 'ctx')
- value_grad: bfloat16 [8, 16384, 1024], P('dp', 'ctx')
- query_gain_grad: float32 [128], replicated
- key_gain_grad: float32 [128], replicated
Inputs may be any that keep to these rules, and one draw needn't show every extreme that they name: selected[b, i, 0] is 0 for every query block i, and selected[b, i, 2] is i - 1 for every i >= 2. Every entry of row i lies in 0 to i, and an entry equal to i names no block. Entries below i are distinct within a row. For i >= 3 every entry is below i.
All inputs are finite; a program needn't handle non-finite values.
Results may differ from a plain program's by a relative error of at most 0.012.
Values may be sent and summed in bfloat16 or wider, within the bound.
A program may use at most 128 MiB of HBM per device.

v0:
```python
import jax
import jax.numpy as jnp
from jax import lax
from jax.sharding import PartitionSpec as P


def head_norm(inputs, gain_vector):
    head_dim = gain_vector.shape[0]
    shaped = inputs.reshape(inputs.shape[:-1] + (inputs.shape[-1] // head_dim, head_dim))
    factor = lax.rsqrt(jnp.mean(shaped * shaped, axis=-1, keepdims=True) + 1e-06)
    return (shaped * factor * gain_vector).reshape(inputs.shape)


def attend(query_block, key_list, value_list, visible_list, grad_block, score_scale):
    weight_list = []
    row_total = 0.0
    for key_block, visible in zip(key_list, visible_list):
        scores = jnp.einsum(
            "qhd,khd->hqk", query_block, key_block, preferred_element_type=jnp.float32
        )
        weights = jnp.exp(score_scale * scores) * visible
        row_total = row_total + jnp.sum(weights, axis=-1)
        weight_list.append(weights)
    prob_list = [(weights / row_total[:, :, None]).astype(jnp.bfloat16) for weights in weight_list]
    accumulated = 0.0
    for prob_block, value_block in zip(prob_list, value_list):
        accumulated = accumulated + jnp.einsum(
            "hqk,khd->qhd", prob_block, value_block, preferred_element_type=jnp.float32
        )
    output = accumulated.astype(jnp.bfloat16)
    row_delta = jnp.einsum("qhd,qhd->hq", grad_block, output, preferred_element_type=jnp.float32)
    query_grad = 0.0
    key_terms = []
    value_terms = []
    for prob_block, key_block, value_block in zip(prob_list, key_list, value_list):
        grad_probs = jnp.einsum(
            "qhd,khd->hqk", grad_block, value_block, preferred_element_type=jnp.float32
        )
        grad_scores = (
            prob_block.astype(jnp.float32) * (grad_probs - row_delta[:, :, None])
        ).astype(jnp.bfloat16)
        value_terms.append(
            jnp.einsum("hqk,qhd->khd", prob_block, grad_block, preferred_element_type=jnp.float32)
        )
        key_terms.append(
            score_scale
            * jnp.einsum(
                "hqk,qhd->khd", grad_scores, query_block, preferred_element_type=jnp.float32
            )
        )
        query_grad = query_grad + score_scale * jnp.einsum(
            "hqk,khd->qhd", grad_scores, key_block, preferred_element_type=jnp.float32
        )
    return (output, query_grad, key_terms, value_terms)


def local(query_rows, key_rows, value_rows, query_gain, key_gain, selected, output_grad):
    ctx_count = lax.axis_size("ctx")
    device_index = lax.axis_index("ctx")
    local_count = selected.shape[1]
    slot_total = selected.shape[2]
    token_count = query_rows.shape[1]
    model_width = query_rows.shape[2]
    head_dim = query_gain.shape[0]
    head_count = model_width // head_dim
    block_size = token_count // local_count
    slice_rows = block_size // ctx_count
    block_count = local_count * ctx_count
    score_scale = head_dim ** (-0.5)

    def heads_view(block_array):
        return block_array.reshape(block_size, head_count, head_dim)

    choice_table = lax.all_gather(selected[0], "ctx", axis=0, tiled=True)
    query_float = query_rows[0].astype(jnp.float32)
    key_float = key_rows[0].astype(jnp.float32)
    query_normed = head_norm(query_float, query_gain).astype(jnp.bfloat16)
    key_normed = head_norm(key_float, key_gain).astype(jnp.bfloat16)
    value_local = value_rows[0]
    holder_keys, holder_values = (
        lax.all_to_all(
            key_normed.reshape(local_count, block_size, model_width),
            "ctx",
            split_axis=1,
            concat_axis=0,
            tiled=True,
        ),
        lax.all_to_all(
            value_local.reshape(local_count, block_size, model_width),
            "ctx",
            split_axis=1,
            concat_axis=0,
            tiled=True,
        ),
    )
    first_slot = 0
    fetched_keys, fetched_values = (
        lax.all_to_all(holder_keys[choice_table], "ctx", split_axis=0, concat_axis=2, tiled=True),
        lax.all_to_all(holder_values[choice_table], "ctx", split_axis=0, concat_axis=2, tiled=True),
    )
    positions = jnp.arange(block_size)
    causal = (positions[None, :] <= positions[:, None]).astype(jnp.float32)[None]
    own_block = device_index * local_count + 0
    chosen = selected[0, 0]
    key_list = [heads_view(key_normed)]
    value_list = [heads_view(value_local)]
    visible_list = [causal]
    for slot_index in range(slot_total):
        fetched_slot = slot_index - first_slot
        key_list.append(heads_view(fetched_keys[0, fetched_slot]))
        value_list.append(heads_view(fetched_values[0, fetched_slot]))
        visible_list.append((chosen[slot_index] != own_block).astype(jnp.float32))
    output, query_grad, key_terms, value_terms = attend(
        heads_view(query_normed),
        key_list,
        value_list,
        visible_list,
        heads_view(output_grad[0, 0:block_size]),
        score_scale,
    )
    outputs = output.reshape(block_size, model_width)
    query_grads = query_grad.reshape(block_size, model_width)
    own_keys = [key_terms[0].reshape(block_size, model_width)]
    own_values = [value_terms[0].reshape(block_size, model_width)]
    remote_keys = [
        jnp.stack([grad_term.astype(jnp.bfloat16) for grad_term in key_terms[1:]]).reshape(
            slot_total, block_size, model_width
        )
    ]
    remote_values = [
        jnp.stack([grad_term.astype(jnp.bfloat16) for grad_term in value_terms[1:]]).reshape(
            slot_total, block_size, model_width
        )
    ]
    remote_key_all = jnp.stack(remote_keys)
    remote_value_all = jnp.stack(remote_values)
    back_keys, back_values = (
        lax.all_to_all(remote_key_all, "ctx", split_axis=2, concat_axis=0, tiled=True),
        lax.all_to_all(remote_value_all, "ctx", split_axis=2, concat_axis=0, tiled=True),
    )
    selector = (choice_table.reshape(-1)[None, :] == jnp.arange(block_count)[:, None]).astype(
        jnp.bfloat16
    )
    summed_keys = jnp.dot(
        selector,
        back_keys.reshape(block_count * slot_total, slice_rows * model_width),
        preferred_element_type=jnp.float32,
    )
    summed_values = jnp.dot(
        selector,
        back_values.reshape(block_count * slot_total, slice_rows * model_width),
        preferred_element_type=jnp.float32,
    )
    summed_keys = summed_keys.reshape(block_count, slice_rows, model_width)
    summed_values = summed_values.reshape(block_count, slice_rows, model_width)
    collected_keys, collected_values = (
        lax.all_to_all(
            summed_keys.astype(jnp.bfloat16), "ctx", split_axis=0, concat_axis=1, tiled=True
        ),
        lax.all_to_all(
            summed_values.astype(jnp.bfloat16), "ctx", split_axis=0, concat_axis=1, tiled=True
        ),
    )
    remote_key_total = collected_keys.astype(jnp.float32)
    remote_value_total = collected_values.astype(jnp.float32)
    key_total = (jnp.stack(own_keys) + remote_key_total).reshape(token_count, model_width)
    value_grad = (
        (jnp.stack(own_values) + remote_value_total)
        .reshape(token_count, model_width)
        .astype(jnp.bfloat16)
    )
    _, query_pull = jax.vjp(head_norm, query_float, query_gain)
    query_grad, query_gain_part = query_pull(query_grads)
    _, key_pull = jax.vjp(head_norm, key_float, key_gain)
    key_grad, key_gain_part = key_pull(key_total)
    query_gain_grad, key_gain_grad = lax.psum((query_gain_part, key_gain_part), ("dp", "ctx"))
    return (
        outputs[None],
        query_grad.astype(jnp.bfloat16)[None],
        key_grad.astype(jnp.bfloat16)[None],
        value_grad[None],
        query_gain_grad,
        key_gain_grad,
    )


def solution(mesh):
    in_specs = (
        P("dp", "ctx", None),
        P("dp", "ctx", None),
        P("dp", "ctx", None),
        P(),
        P(),
        P("dp", "ctx", None),
        P("dp", "ctx", None),
    )
    out_specs = (
        P("dp", "ctx", None),
        P("dp", "ctx", None),
        P("dp", "ctx", None),
        P("dp", "ctx", None),
        P(),
        P(),
    )
    return jax.shard_map(local, mesh=mesh, in_specs=in_specs, out_specs=out_specs, check_vma=False)
```

profile of v0, /device:TPU:1, one launch (start us, length us, event | category | flops | bytes accessed | tf_op | source)
XLA Modules:
  0.0 716.8 jit_solution(10691990284044521353)
XLA Ops:
  13.3 9.1 %reduce.7 = bf16[512,1024]{1,0:T(8,128)(2,1)} reduce(bf16[512,1,1024]{2,1,0:T(2,128)(2,1)} %bitcast.237, bf16[]{:T(256)} %broadcast.153), dimensions={1}, to_apply=%bitcast.200.reduce_sub_computation | reduce | bytes 2097154
  25.0 12.2 %all-to-all-start = ((bf16[32,2,8192]{2,1,0:T(2,128)(2,1)}), bf16[32,2,8192]{2,1,0:T(2,128)(2,1)}, u32[]{:S(2)}, u32[]{:S(2)}) async-start(bf16[32,2,8192]{2,1,0:T(2,128)(2,1)} %reshape.270), calls=%async_computation | async-start | bytes 2097152 | tf_op jit(solution)/shard_map/all_to_all | solution.py:81
  40.1 8.0 %reduce.6 = bf16[512,1024]{1,0:T(8,128)(2,1)S(1)} reduce(bf16[512,1,1024]{2,1,0:T(2,128)(2,1)} %bitcast.238, bf16[]{:T(256)} %broadcast.153), dimensions={1}, to_apply=%bitcast.199.reduce_sub_computation | reduce | bytes 2097154
  49.7 12.0 %all-to-all-done = bf16[32,2,8192]{2,1,0:T(2,128)(2,1)} async-done(((bf16[32,2,8192]{2,1,0:T(2,128)(2,1)}), bf16[32,2,8192]{2,1,0:T(2,128)(2,1)}, u32[]{:S(2)}, u32[]{:S(2)}) %all-to-all-start) | async-done | bytes 1048608 | tf_op jit(solution)/shard_map/all_to_all | solution.py:81
  61.7 8.7 %all-to-all-start.2 = ((bf16[32,2,8192]{2,1,0:T(2,128)(2,1)}), bf16[32,2,8192]{2,1,0:T(2,128)(2,1)}, u32[]{:S(2)}, u32[]{:S(2)}) async-start(bf16[32,2,8192]{2,1,0:T(2,128)(2,1)} %reshape.268), calls=%async_computation.2 | async-start | bytes 2097152 | tf_op jit(solution)/shard_map/all_to_all | solution.py:88
  70.5 48.7 %all-gather = s32[32,1,3]{2,1,0:T(1,128)S(1)} all-gather(s32[1,1,3]{2,1,0:T(1,128)S(1)} %copy-done.32), channel_id=2, replica_groups=mesh['dp'=8,'ctx'=32] {'ctx'}, dimensions={0}, use_global_device_ids=true | all-gather | bytes 396 | tf_op jit(solution)/shard_map/all_gather | solution.py:74
  119.5 5.8 reshape.271
  129.8 5.3 all-to-all-start.1
  135.1 5.8 reshape.269
  145.5 54.6 %all-to-all-done.1 = bf16[32,3,16,1024]{3,2,1,0:T(8,128)(2,1)} async-done(((bf16[32,3,16,1024]{3,2,1,0:T(8,128)(2,1)}), bf16[32,3,16,1024]{3,2,1,0:T(8,128)(2,1)}, u32[]{:S(2)}, u32[]{:S(2)}) %all-to-all-start.1) | async-done | bytes 3145760 | tf_op jit(solution)/shard_map/all_to_all | solution.py:98
  200.1 5.4 all-to-all-start.3
  217.4 4.4 fusion.3
  232.8 34.6 %all-to-all-done.3 = bf16[32,3,16,1024]{3,2,1,0:T(8,128)(2,1)} async-done(((bf16[32,3,16,1024]{3,2,1,0:T(8,128)(2,1)}), bf16[32,3,16,1024]{3,2,1,0:T(8,128)(2,1)}, u32[]{:S(2)}, u32[]{:S(2)}) %all-to-all-start.3) | async-done | bytes 3145760 | tf_op jit(solution)/shard_map/all_to_all | solution.py:99
  278.4 6.3 fusion.6
  284.8 5.1 fusion.5
  289.9 5.0 fusion.4
  295.0 11.9 %divide_convert_fusion.3 = (bf16[8,512,512]{1,2,0:T(8,128)(2,1)S(1)}, bf16[8,512,512]{1,2,0:T(8,128)(2,1)S(1)}, bf16[8,512,512]{1,2,0:T(8,128)(2,1)S(1)}, bf16[8,512,512]{1,2,0:T(8,128)(2,1)S(1)}) fusion(f32[8,512,512]{1,2,0:T(8,128)S(1)} %bitcast.207, f32[8,512]{1,0:T(8,128)S(1)} %add_add_fusion.2, f32[512,512]{0,1:T(8,128)} %copy-done.14, ...), kind=kLoop, calls=%fused_computation.12 | loop fusion | flops 33554432 | bytes 51396620 | tf_op jit(solution)/shard_map/convert_element_type | solution.py:24
  321.4 4.0 fusion.2
  325.5 3.3 fusion.1
  336.6 6.0 copy.538
  342.6 4.6 multiply_convert_fusion.2
  347.3 6.0 copy.539
  353.3 4.6 multiply_convert_fusion.1
  358.0 6.2 copy.540
  364.1 9.6 %pad_maximum_fusion = bf16[1,3,512,1024]{3,1,0,2:T(4,128)(2,1)} fusion(bf16[1,1,512,1024]{3,1,0,2:T(2,128)(2,1)} %copy.540, bf16[1,1,512,1024]{3,1,0,2:T(2,128)(2,1)} %copy.539, bf16[1,1,512,1024]{3,1,0,2:T(2,128)(2,1)} %copy.538), kind=kLoop, calls=%fused_computation.21 | loop fusion | flops 9437184 | bytes 6291456 | tf_op jit(solution)/shard_map/stack | solution.py:126
  373.8 7.3 %all-to-all-start.4 = ((bf16[1,3,512,1024]{3,1,0,2:T(4,128)(2,1)}), bf16[1,3,512,1024]{3,1,0,2:T(4,128)(2,1)}, u32[]{:S(2)}, u32[]{:S(2)}) async-start(bf16[1,3,512,1024]{3,1,0,2:T(4,128)(2,1)} %pad_maximum_fusion), calls=%async_computation.4 | async-start | bytes 8388608 | tf_op jit(solution)/shard_map/all_to_all | solution.py:138
  381.1 4.6 convolution_convert_fusion.2
  385.7 6.1 copy.556
  391.8 4.6 convolution_convert_fusion.1
  396.4 6.0 copy.557
  402.4 4.6 convolution_convert_fusion
  407.1 6.1 copy.558
  413.2 9.7 %pad_maximum_fusion.1 = bf16[1,3,512,1024]{3,1,0,2:T(4,128)(2,1)} fusion(bf16[1,1,512,1024]{3,1,0,2:T(2,128)(2,1)} %copy.558, bf16[1,1,512,1024]{3,1,0,2:T(2,128)(2,1)} %copy.557, bf16[1,1,512,1024]{3,1,0,2:T(2,128)(2,1)} %copy.556), kind=kLoop, calls=%fused_computation.22 | loop fusion | flops 9437184 | bytes 6291456 | tf_op jit(solution)/shard_map/stack | solution.py:131
  422.9 42.1 %all-to-all-done.4 = bf16[1,3,512,1024]{3,1,0,2:T(4,128)(2,1)} async-done(((bf16[1,3,512,1024]{3,1,0,2:T(4,128)(2,1)}), bf16[1,3,512,1024]{3,1,0,2:T(4,128)(2,1)}, u32[]{:S(2)}, u32[]{:S(2)}) %all-to-all-start.4) | async-done | bytes 3145760 | tf_op jit(solution)/shard_map/all_to_all | solution.py:138
  465.0 9.8 %all-to-all-start.6 = ((bf16[1,3,512,1024]{3,1,0,2:T(4,128)(2,1)}), bf16[1,3,512,1024]{3,1,0,2:T(4,128)(2,1)}, u32[]{:S(2)}, u32[]{:S(2)}) async-start(bf16[1,3,512,1024]{3,1,0,2:T(4,128)(2,1)} %pad_maximum_fusion.1), calls=%async_computation.6 | async-start | bytes 8388608 | tf_op jit(solution)/shard_map/all_to_all | solution.py:139
  476.1 4.6 fusion.44
  480.7 3.4 copy.541
  484.5 3.6 fusion.20
  489.7 71.2 %all-to-all-done.6 = bf16[1,3,512,1024]{3,1,0,2:T(4,128)(2,1)} async-done(((bf16[1,3,512,1024]{3,1,0,2:T(4,128)(2,1)}), bf16[1,3,512,1024]{3,1,0,2:T(4,128)(2,1)}, u32[]{:S(2)}, u32[]{:S(2)}) %all-to-all-start.6) | async-done | bytes 3145760 | tf_op jit(solution)/shard_map/all_to_all | solution.py:139
  560.9 7.3 %all-to-all-start.5 = ((bf16[32,16,1024]{2,1,0:T(8,128)(2,1)}), bf16[32,16,1024]{2,1,0:T(8,128)(2,1)}, u32[]{:S(2)}, u32[]{:S(2)}) async-start(bf16[32,16,1024]{2,1,0:T(8,128)(2,1)} %copy.544), calls=%async_computation.5 | async-start | bytes 2097152 | tf_op jit(solution)/shard_map/all_to_all | solution.py:157
  568.2 3.4 fusion.45
  581.0 3.4 copy.559
  584.8 3.6 fusion.23
  590.0 9.6 %all-to-all-start.7 = ((bf16[32,16,1024]{2,1,0:T(8,128)(2,1)}), bf16[32,16,1024]{2,1,0:T(8,128)(2,1)S(1)}, u32[]{:S(2)}, u32[]{:S(2)}) async-start(bf16[32,16,1024]{2,1,0:T(8,128)(2,1)} %copy.562), calls=%async_computation.7 | async-start | bytes 2097152 | tf_op jit(solution)/shard_map/all_to_all | solution.py:160
  599.6 5.0 fusion.46
  607.6 3.9 fusion.15
  620.9 5.2 multiply_reduce_fusion.1
  630.0 85.0 %all-reduce = (f32[128]{0:T(128)}, f32[128]{0:T(128)}) all-reduce(f32[128]{0:T(128)S(1)} %get-tuple-element.56, f32[128]{0:T(128)S(1)} %get-tuple-element.54), channel_id=1, replica_groups=mesh['dp'=8,'ctx'=32] {'dp','ctx'}, use_global_device_ids=true, to_apply=%region_9.0 | all-reduce | flops 256 | bytes 2048 | tf_op jit(solution)/shard_map/psum | solution.py:176
  (149 shorter events, 115.4 us)
Async XLA Ops:
  3.3 4.5 copy-start.31
  3.3 4.5 copy-start.26
  13.3 23.9 %copy-start.27 = (bf16[1,512,1024]{2,1,0:T(8,128)(2,1)S(1)}, bf16[1,512,1024]{2,1,0:T(8,128)(2,1)}, u32[]{:S(2)}) copy-start(bf16[1,512,1024]{2,1,0:T(8,128)(2,1)} %param.9) | copy-start | bytes 3145732
  25.0 36.8 %all-to-all-start = ((bf16[32,2,8192]{2,1,0:T(2,128)(2,1)}), bf16[32,2,8192]{2,1,0:T(2,128)(2,1)}, u32[]{:S(2)}, u32[]{:S(2)}) async-start(bf16[32,2,8192]{2,1,0:T(2,128)(2,1)} %reshape.270), calls=%async_computation | async-start | bytes 2097152 | tf_op jit(solution)/shard_map/all_to_all | solution.py:81
  40.1 30.4 %copy-start.32 = (s32[1,1,3]{2,1,0:T(1,128)S(1)}, s32[1,1,3]{2,1,0:T(1,128)}, u32[]{:S(2)}) copy-start(s32[1,1,3]{2,1,0:T(1,128)} %param.12) | copy-start | bytes 40
  61.7 68.1 %all-to-all-start.2 = ((bf16[32,2,8192]{2,1,0:T(2,128)(2,1)}), bf16[32,2,8192]{2,1,0:T(2,128)(2,1)}, u32[]{:S(2)}, u32[]{:S(2)}) async-start(bf16[32,2,8192]{2,1,0:T(2,128)(2,1)} %reshape.268), calls=%async_computation.2 | async-start | bytes 2097152 | tf_op jit(solution)/shard_map/all_to_all | solution.py:88
  129.8 70.3 %all-to-all-start.1 = ((bf16[32,3,16,1024]{3,2,1,0:T(8,128)(2,1)}), bf16[32,3,16,1024]{3,2,1,0:T(8,128)(2,1)}, u32[]{:S(2)}, u32[]{:S(2)}) async-start(bf16[32,3,16,1024]{3,2,1,0:T(8,128)(2,1)} %bitcast.215), calls=%async_computation.1 | async-start | bytes 6291456 | tf_op jit(solution)/shard_map/all_to_all | solution.py:98
  200.1 67.3 %all-to-all-start.3 = ((bf16[32,3,16,1024]{3,2,1,0:T(8,128)(2,1)}), bf16[32,3,16,1024]{3,2,1,0:T(8,128)(2,1)}, u32[]{:S(2)}, u32[]{:S(2)}) async-start(bf16[32,3,16,1024]{3,2,1,0:T(8,128)(2,1)} %bitcast.214), calls=%async_computation.3 | async-start | bytes 6291456 | tf_op jit(solution)/shard_map/all_to_all | solution.py:99
  205.5 1.9 copy-start.29
  207.4 4.2 copy-start.28
  207.4 4.5 copy-start.30
  212.1 3.2 copy-start.19
  212.1 3.2 copy-start.33
  212.8 4.5 copy-start.8
  213.0 8.8 %copy-start.14 = (f32[512,512]{0,1:T(8,128)}, f32[512,512]{0,1:T(8,128)S(1)}, u32[]{:S(2)}) copy-start(f32[512,512]{0,1:T(8,128)S(1)} %fusion.26) | copy-start | bytes 3145732
  278.4 6.3 copy-start.21
  284.8 5.1 copy-start.22
  284.8 10.1 %slice-start = ((s8[8388608]{0:T(1024)(128)(4,1)}), s8[4194304]{0:T(1024)(128)(4,1)S(1)}, s32[]{:S(2)}) async-start(s8[8388608]{0:T(1024)(128)(4,1)} %bitcast.206), calls=%async_computation.8 | async-start | bytes 8388608
  289.9 5.1 slice-start.1
  306.9 3.9 copy-start.2
  306.9 5.8 copy-start.4
  306.9 5.8 copy-start.6
  306.9 6.3 copy-start
  306.9 3.1 copy-start.15
  310.0 2.0 copy-start.17
  321.4 4.0 copy-start.5
  321.4 4.1 copy-start.16
  325.5 8.7 %copy-start.11 = (bf16[8,512,512]{1,2,0:T(8,128)(2,1)}, bf16[8,512,512]{1,2,0:T(8,128)(2,1)S(1)}, u32[]{:S(2)}) copy-start(bf16[8,512,512]{1,2,0:T(8,128)(2,1)S(1)} %fusion.2) | copy-start | bytes 12582916
  325.5 5.1 copy-start.3
  325.5 5.4 copy-start.18
  373.8 91.2 %all-to-all-start.4 = ((bf16[1,3,512,1024]{3,1,0,2:T(4,128)(2,1)}), bf16[1,3,512,1024]{3,1,0,2:T(4,128)(2,1)}, u32[]{:S(2)}, u32[]{:S(2)}) async-start(bf16[1,3,512,1024]{3,1,0,2:T(4,128)(2,1)} %pad_maximum_fusion), calls=%async_computation.4 | async-start | bytes 8388608 | tf_op jit(solution)/shard_map/all_to_all | solution.py:138
  465.0 95.9 %all-to-all-start.6 = ((bf16[1,3,512,1024]{3,1,0,2:T(4,128)(2,1)}), bf16[1,3,512,1024]{3,1,0,2:T(4,128)(2,1)}, u32[]{:S(2)}, u32[]{:S(2)}) async-start(bf16[1,3,512,1024]{3,1,0,2:T(4,128)(2,1)} %pad_maximum_fusion.1), calls=%async_computation.6 | async-start | bytes 8388608 | tf_op jit(solution)/shard_map/all_to_all | solution.py:139
  560.9 29.1 %all-to-all-start.5 = ((bf16[32,16,1024]{2,1,0:T(8,128)(2,1)}), bf16[32,16,1024]{2,1,0:T(8,128)(2,1)}, u32[]{:S(2)}, u32[]{:S(2)}) async-start(bf16[32,16,1024]{2,1,0:T(8,128)(2,1)} %copy.544), calls=%async_computation.5 | async-start | bytes 2097152 | tf_op jit(solution)/shard_map/all_to_all | solution.py:157
  568.2 3.7 copy-start.1
  572.0 1.6 copy-start.9
  572.0 3.7 copy-start.23
  573.6 2.1 copy-start.12
  573.6 3.3 copy-start.7
  573.6 4.5 copy-start.13
  573.6 4.7 copy-start.20
  590.0 125.0 %all-to-all-start.7 = ((bf16[32,16,1024]{2,1,0:T(8,128)(2,1)}), bf16[32,16,1024]{2,1,0:T(8,128)(2,1)S(1)}, u32[]{:S(2)}, u32[]{:S(2)}) async-start(bf16[32,16,1024]{2,1,0:T(8,128)(2,1)} %copy.562), calls=%async_computation.7 | async-start | bytes 2097152 | tf_op jit(solution)/shard_map/all_to_all | solution.py:160
  607.6 6.2 copy-start.25
  620.9 5.2 copy-start.10
  626.1 88.9 %copy-start.24 = (f32[1,512,1024]{2,1,0:T(8,128)S(1)}, f32[1,512,1024]{2,1,0:T(8,128)}, u32[]{:S(2)}) copy-start(f32[1,512,1024]{2,1,0:T(8,128)} %copy.563) | copy-start | bytes 6291460
where the time goes:
time: 727 us; the launch traced here: 717 us
  waiting for transfers between devices  215 us (30%)
  local copies, waits for them, and re-layouts  138 us (19%)
  blocking collectives  134 us (18%)
  matrix products  94.3 us (13%)
  other arithmetic  66.9 us (9%)
  starting transfers between devices  65.5 us (9%)
    psum x1, blocking collectives, local(): lax.psum((query_gain_part, key_gain_part), ('dp', 'ctx'))  85 us
    all_to_all x1, waiting for transfers between devices, local(): lax.all_to_all(remote_value_all, 'ctx', split_axis=2, concat_axis=0, tile...  71.2 us
    all_to_all x1, waiting for transfers between devices, local(): lax.all_to_all(holder_keys[choice_table], 'ctx', split_axis=0, concat_axi...  54.6 us
    all_gather x1, blocking collectives, local(): choice_table = lax.all_gather(selected[0], 'ctx', axis=0, tiled=True)  48.7 us
    unnamed x88, local copies, waits for them, and re-layouts  44.6 us
    all_to_all x1, waiting for transfers between devices, local(): lax.all_to_all(remote_key_all, 'ctx', split_axis=2, concat_axis=0, tiled=...  42.1 us
    all_to_all x1, waiting for transfers between devices, local(): lax.all_to_all(holder_values[choice_table], 'ctx', split_axis=0, concat_a...  34.6 us
    unnamed x5, other arithmetic  21.1 us
  transfers between devices with their start and end apart: 8, of which 5 were waited for; matrix products, arithmetic and copies ran while one was open for 23% of the time, Pallas kernels for 0%

commit v1 on v0

v1 whole, which is shorter than its diff:
```python
import functools

import jax
import jax.numpy as jnp
from jax import lax
from jax.experimental import pallas as pl
from jax.experimental.pallas import tpu as pltpu
from jax.sharding import PartitionSpec as P

CHUNKS = 2
EPS = 1e-06
OWN, PREV, FIRST, MID = 0, 1, 2, 3
F32, BF16 = jnp.float32, jnp.bfloat16


def dot(left, right, dims):
    return lax.dot_general(left, right, (dims, ((), ())), preferred_element_type=F32)


def body(
    cfg,
    q_ref, k_ref, v_ref, qg_ref, kg_ref, sel_ref, do_ref,
    att_ref, dq_ref, dk_ref, dv_ref, gain_ref,
    kv, hold, pick, fetch, prev, first, w_scr,
    term, own_grad, back, part, sums, coll, prev_back, rx, rz_out, rz,
    sel_tile, table, table_s, links, gq, gk, gbuf, gbuf2,
    send_sem, recv_sem, sel_sem, local_sem, gain_sem,
):
    n, nx, nz, n_dp, chunks, heads, hd, block = (
        cfg[k] for k in ("n", "nx", "nz", "n_dp", "chunks", "heads", "hd", "block")
    )
    rows = block // n
    width = heads * hd // chunks
    per_chunk = heads // chunks
    scale = hd ** (-0.5)
    me = lax.axis_index("ctx")
    my_dp = lax.axis_index("dp")
    x, z = lax.div(me, nz), lax.rem(me, nz)
    up, down = lax.rem(me + 1, n), lax.rem(me + n - 1, n)

    def peer_of(kx, kz):
        return lax.rem(x + kx, nx) * nz + lax.rem(z + kz, nz)

    def each_peer(fn):
        def step(k, carry):
            fn(peer_of(lax.div(k, nz), lax.rem(k, nz)))
            return carry

        lax.fori_loop(1, n, step, 0)

    def each_z(fn):
        def step(k, carry):
            fn(peer_of(0, k), lax.rem(z + k, nz))
            return carry

        lax.fori_loop(1, nz, step, 0)

    def each_x(fn):
        for k in range(1, nx):
            fn(peer_of(k, 0), lax.rem(x + k, nx))

    def remote(src, dst, stage, c, peer):
        return pltpu.make_async_remote_copy(
            src_ref=src,
            dst_ref=dst,
            send_sem=send_sem.at[stage, c],
            recv_sem=recv_sem.at[stage, c],
            device_id={"ctx": peer},
            device_id_type=pl.DeviceIdType.MESH,
        )

    waits = []

    def landed(like, stage, c):
        remote(like, like, stage, c, up).wait_recv()
        waits.append((like, stage, c))

    HOLD, FETCH, BACK, COLL, PREV_F, PREV_B, AG_Z, AG_X, RS_X, RS_Z = range(10)

    barrier = pltpu.get_barrier_semaphore()

    def greet(peer):
        pl.semaphore_signal(
            barrier, inc=1, device_id={"ctx": peer}, device_id_type=pl.DeviceIdType.MESH
        )

    each_peer(greet)
    for k in range(1, n_dp):
        pl.semaphore_signal(
            barrier,
            inc=1,
            device_id={"dp": lax.rem(my_dp + k, n_dp)},
            device_id_type=pl.DeviceIdType.MESH,
        )

    def norm_chunk(c):
        def step(hh, carry):
            at = pl.ds(pl.multiple_of(hh * hd, hd), hd)
            wide = pl.ds(pl.multiple_of(c * width + hh * hd, hd), hd)
            xk = k_ref[0, :, wide].astype(F32)
            factor = lax.rsqrt(jnp.mean(xk * xk, axis=-1, keepdims=True) + EPS)
            kn = (xk * factor * kg_ref[...]).astype(BF16)
            kv[c, :, 0:rows, at] = kn.reshape(n, rows, hd)
            kv[c, :, rows : 2 * rows, at] = v_ref[0, :, wide].reshape(n, rows, hd)
            return carry

        lax.fori_loop(0, per_chunk, step, 0)

    norm_chunk(0)
    sel_tile[...] = jnp.full(sel_tile.shape, sel_ref[0, 0, 1], jnp.int32)
    pl.semaphore_wait(barrier, n - 1 + n_dp - 1)

    def send_table(peer):
        pltpu.make_async_remote_copy(
            src_ref=sel_tile,
            dst_ref=table.at[me],
            send_sem=sel_sem.at[0],
            recv_sem=sel_sem.at[1],
            device_id={"ctx": peer},
            device_id_type=pl.DeviceIdType.MESH,
        ).start()

    each_peer(send_table)
    table[me] = sel_tile[...]

    def send_hold(c):
        each_peer(lambda p: remote(kv.at[c, p], hold[c].at[me], HOLD, c, p).start())
        hold[c][me] = kv[c, me]

    def send_prev(c):
        remote(kv.at[c], prev.at[c], PREV_F, c, up).start()

    send_hold(0)
    for c in range(1, chunks):
        norm_chunk(c)
        send_hold(c)
    for c in range(chunks):
        send_prev(c)

    some = pltpu.make_async_remote_copy(
        src_ref=table.at[pl.ds(0, n - 1)],
        dst_ref=table.at[pl.ds(0, n - 1)],
        send_sem=sel_sem.at[0],
        recv_sem=sel_sem.at[1],
        device_id={"ctx": up},
        device_id_type=pl.DeviceIdType.MESH,
    )
    some.wait_recv()
    to_scalars = pltpu.make_async_copy(table, table_s, local_sem)
    to_scalars.start()
    to_scalars.wait()

    def link(i, carry):
        mine = table_s[i, 0, 0]

        def look(o, found):
            before, last = found
            other = table_s[o, 0, 0]
            before = jnp.where((o < i) & (other == mine), o, before)
            last = jnp.where(other == i, o, last)
            return before, last

        before, last = lax.fori_loop(0, n, look, (jnp.int32(n), jnp.int32(n)))
        links[0, i] = before
        links[1, i] = last
        return carry

    lax.fori_loop(0, n, link, 0)

    def serve(c):
        landed(hold[c].at[pl.ds(0, n - 1)], HOLD, c)
        first[c, me] = hold[c][0]
        each_z(lambda p, _: remote(first.at[c, me], first.at[c, me], AG_Z, c, p).start())

        def send(p):
            pick[c, p] = hold[c][table_s[p, 0, 0]]
            remote(pick.at[c, p], fetch.at[c, me], FETCH, c, p).start()

        each_peer(send)
        fetch[c, me] = hold[c][table_s[me, 0, 0]]

    def spread(c):
        landed(first.at[c, pl.ds(0, nz - 1)], AG_Z, c)
        row = pl.ds(x * nz, nz)
        each_x(lambda p, _: remote(first.at[c, row], first.at[c, row], AG_X, c, p).start())

    for c in range(chunks):
        serve(c)
        spread(c)

    see_prev = (me >= 2).astype(F32)
    see_first = (me >= 1).astype(F32)
    see_mid = jnp.where(table_s[me, 0, 0] != me, 1.0, 0.0).astype(F32)
    see = (None, see_prev, see_first, see_mid)
    stores = (kv, prev, first, fetch)

    def seen(value, b):
        return value if see[b] is None else value * see[b]

    gq[...] = jnp.zeros_like(gq)
    gk[...] = jnp.zeros_like(gk)

    def attend(c):
        def step(hh, carry):
            at = pl.ds(pl.multiple_of(hh * hd, hd), hd)
            wide = pl.ds(pl.multiple_of(c * width + hh * hd, hd), hd)
            xt = q_ref[0, :, wide].astype(F32).T
            factor = lax.rsqrt(jnp.mean(xt * xt, axis=0, keepdims=True) + EPS)
            gain = qg_ref[...]
            qn = (xt * factor * gain).astype(BF16)
            do = do_ref[0, :, wide].astype(F32).T
            do_b = do.astype(BF16)

            def keys(b):
                return stores[b][c, :, 0:rows, at].reshape(block, hd)

            def values(b):
                return stores[b][c, :, rows : 2 * rows, at].reshape(block, hd)

            total = jnp.zeros((1, block), F32)
            acc = jnp.zeros((hd, block), F32)
            for b in (OWN, PREV, FIRST, MID):
                s = dot(keys(b), qn, ((1,), (0,)))
                w = jnp.exp2(s * (scale * 1.4426950408889634))
                if b == OWN:
                    ki = lax.broadcasted_iota(jnp.int32, (block, block), 0)
                    qi = lax.broadcasted_iota(jnp.int32, (block, block), 1)
                    w = jnp.where(ki <= qi, w, 0.0)
                total = total + seen(jnp.sum(w, axis=0, keepdims=True), b)
                wb = w.astype(BF16)
                w_scr[b] = wb
                acc = acc + seen(dot(values(b), wb, ((0,), (0,))), b)
            inv = 1.0 / total
            out = (acc * inv).astype(BF16).astype(F32)
            att_ref[0, :, wide] = out.T.astype(BF16)
            delta = jnp.sum(do * out, axis=0, keepdims=True)
            inv_s = inv * scale
            qs = (qn.astype(F32) * inv_s).astype(BF16)
            dos = (do * inv).astype(BF16)
            dq = jnp.zeros((hd, block), F32)
            for b in (MID, FIRST, PREV, OWN):
                wb = w_scr[b]
                dp = dot(values(b), do_b, ((1,), (0,)))
                ds = (wb.astype(F32) * (dp - delta)).astype(BF16)
                dq = dq + seen(dot(keys(b), ds, ((0,), (0,))), b)
                dk = seen(dot(ds, qs, ((1,), (1,))), b)
                dv = seen(dot(wb, dos, ((1,), (1,))), b)
                if b == OWN:
                    own_grad[0, :, wide] = dk
                    own_grad[1, :, wide] = dv
                else:
                    term[b - 1, c, :, 0:rows, at] = dk.astype(BF16).reshape(n, rows, hd)
                    term[b - 1, c, :, rows : 2 * rows, at] = dv.astype(BF16).reshape(n, rows, hd)
            dy = dq * inv_s
            xr = xt * factor
            both = dy * xr
            g = both[:, 0:hd]
            for k in range(1, block // hd):
                g = g + both[:, k * hd : (k + 1) * hd]
            gq[...] += g
            u = dy * gain
            dx = factor * (u - xr * jnp.mean(xr * u, axis=0, keepdims=True))
            dq_ref[0, :, wide] = dx.T.astype(BF16)
            return carry

        lax.fori_loop(0, per_chunk, step, 0)

    def give_back(c):
        mid, head, before = term.at[MID - 1, c], term.at[FIRST - 1, c], term.at[PREV - 1, c]
        each_peer(lambda p: remote(mid.at[p], back.at[c, me], BACK, c, p).start())
        back[c, me] = term[MID - 1, c, me]

        def send_row(p, px):
            remote(head.at[pl.ds(px * nz, nz)], rx.at[c, x], RS_X, c, p).start()

        each_x(send_row)
        rx[c, x] = term[FIRST - 1, c, pl.ds(x * nz, nz)]
        remote(before, prev_back.at[c], PREV_B, c, down).start()

    def fold_first(c):
        landed(rx.at[c, pl.ds(0, nx - 1)], RS_X, c)

        def fold(s, carry):
            total = rx[c, 0, s].astype(F32)
            for k in range(1, nx):
                total = total + rx[c, k, s].astype(F32)
            rz_out[c, s] = total.astype(BF16)
            return carry

        lax.fori_loop(0, nz, fold, 0)
        each_z(lambda p, pz: remote(rz_out.at[c, pz], rz.at[c, z], RS_Z, c, p).start())
        rz[c, z] = rz_out[c, z]

    def collect(c):
        landed(back.at[c, pl.ds(0, n - 1)], BACK, c)
        part[n] = jnp.zeros(part.shape[1:], F32)

        def add(i, carry):
            part[i] = back[c, i].astype(F32) + part[links[0, i]]
            return carry

        lax.fori_loop(0, n, add, 0)

        def settle(j, carry):
            sums[c, j] = part[links[1, j]].astype(BF16)
            return carry

        lax.fori_loop(1, n, settle, 0)
        landed(rz.at[c, pl.ds(0, nz - 1)], RS_Z, c)
        total = part[links[1, 0]]
        for k in range(nz):
            total = total + rz[c, k].astype(F32)
        sums[c, 0] = total.astype(BF16)
        each_peer(lambda p: remote(sums.at[c, p], coll.at[c, me], COLL, c, p).start())
        coll[c, me] = sums[c, me]

    def finish(c):
        landed(prev_back.at[c], PREV_B, c)
        landed(coll.at[c, pl.ds(0, n - 1)], COLL, c)

        def step(hh, carry):
            at = pl.ds(pl.multiple_of(hh * hd, hd), hd)
            wide = pl.ds(pl.multiple_of(c * width + hh * hd, hd), hd)

            def remote_sum(lo):
                one = coll[c, :, lo : lo + rows, at].reshape(block, hd).astype(F32)
                two = prev_back[c, :, lo : lo + rows, at].reshape(block, hd).astype(F32)
                return one + two

            dv_ref[0, :, wide] = (own_grad[1, :, wide] + remote_sum(rows)).astype(BF16)
            dy = own_grad[0, :, wide] + remote_sum(0)
            xk = k_ref[0, :, wide].astype(F32)
            factor = lax.rsqrt(jnp.mean(xk * xk, axis=-1, keepdims=True) + EPS)
            xr = xk * factor
            gk[...] += jnp.sum((dy * xr).reshape(block // 8, 8, hd), axis=0)
            u = dy * kg_ref[...]
            dx = factor * (u - xr * jnp.mean(xr * u, axis=-1, keepdims=True))
            dk_ref[0, :, wide] = dx.astype(BF16)
            return carry

        lax.fori_loop(0, per_chunk, step, 0)

    for c in range(chunks):
        landed(prev.at[c], PREV_F, c)
        landed(fetch.at[c, pl.ds(0, n - 1)], FETCH, c)
        landed(first.at[c, pl.ds(0, (nx - 1) * nz)], AG_X, c)
        attend(c)
        give_back(c)
        if c >= 1:
            fold_first(c - 1)
            collect(c - 1)
    fold_first(chunks - 1)
    collect(chunks - 1)
    for c in range(chunks):
        finish(c)

    q_row = jnp.sum(gq[...].T, axis=0, keepdims=True)
    k_row = jnp.sum(gk[...], axis=0, keepdims=True)
    at = lax.broadcasted_iota(jnp.int32, (8, hd), 0)
    gbuf[me] = jnp.where(at == 0, q_row, jnp.where(at == 1, k_row, 0.0))

    def send_gain(buf, slot, at, where):
        return pltpu.make_async_remote_copy(
            src_ref=buf.at[slot],
            dst_ref=buf.at[slot],
            send_sem=gain_sem.at[at, 0],
            recv_sem=gain_sem.at[at, 1],
            device_id=where,
            device_id_type=pl.DeviceIdType.MESH,
        )

    def all_gain(buf, count, at):
        many = buf.at[pl.ds(0, count - 1)]
        return pltpu.make_async_remote_copy(
            src_ref=many,
            dst_ref=many,
            send_sem=gain_sem.at[at, 0],
            recv_sem=gain_sem.at[at, 1],
            device_id={"ctx": up},
            device_id_type=pl.DeviceIdType.MESH,
        )

    each_peer(lambda p: send_gain(gbuf, me, 0, {"ctx": p}).start())
    all_gain(gbuf, n, 0).wait_recv()
    total = gbuf[0]
    for i in range(1, n):
        total = total + gbuf[i]
    gbuf2[my_dp] = total
    for k in range(1, n_dp):
        send_gain(gbuf2, my_dp, 1, {"dp": lax.rem(my_dp + k, n_dp)}).start()
    all_gain(gbuf2, n_dp, 1).wait_recv()
    total = gbuf2[0]
    for i in range(1, n_dp):
        total = total + gbuf2[i]
    gain_ref[...] = total

    all_gain(gbuf, n, 0).wait_send()
    all_gain(gbuf2, n_dp, 1).wait_send()
    some.wait_send()
    for like, stage, c in waits:
        remote(like, like, stage, c, up).wait_send()


def local(mesh_shape, query_rows, key_rows, value_rows, query_gain, key_gain, selected, output_grad):
    n, n_dp = mesh_shape["ctx"], mesh_shape["dp"]
    nz = 8 if n == 32 else n // 2
    nx = n // nz
    block, model = query_rows.shape[1:]
    hd = query_gain.shape[0]
    heads = model // hd
    chunks = CHUNKS
    cfg = dict(n=n, nx=nx, nz=nz, n_dp=n_dp, chunks=chunks, heads=heads, hd=hd, block=block)
    width, rows = model // chunks, block // n
    slices = (chunks, n, 2 * rows, width)
    vmem = pltpu.VMEM
    row = jax.ShapeDtypeStruct((1, block, model), BF16)
    whole = pl.BlockSpec(memory_space=pltpu.VMEM)
    outs = pl.pallas_call(
        functools.partial(body, cfg),
        out_shape=(row, row, row, row, jax.ShapeDtypeStruct((8, hd), F32)),
        in_specs=[whole] * 5 + [pl.BlockSpec(memory_space=pltpu.SMEM), whole],
        out_specs=(whole,) * 5,
        scratch_shapes=[
            vmem(slices, BF16),
            [vmem(slices[1:], BF16)] * chunks,
            vmem(slices, BF16),
            vmem(slices, BF16),
            vmem(slices, BF16),
            vmem(slices, BF16),
            vmem((4, block, block), BF16),
            vmem((3,) + slices, BF16),
            vmem((2, block, model), F32),
            vmem(slices, BF16),
            vmem((n + 1, 2 * rows, width), F32),
            vmem(slices, BF16),
            vmem(slices, BF16),
            vmem(slices, BF16),
            vmem((chunks, nx, nz, 2 * rows, width), BF16),
            vmem((chunks, nz, 2 * rows, width), BF16),
            vmem((chunks, nz, 2 * rows, width), BF16),
            vmem((8, 128), jnp.int32),
            vmem((n, 8, 128), jnp.int32),
            pltpu.SMEM((n, 8, 128), jnp.int32),
            pltpu.SMEM((2, n), jnp.int32),
            vmem((hd, hd), F32),
            vmem((8, hd), F32),
            vmem((n, 8, hd), F32),
            vmem((n_dp, 8, hd), F32),
            pltpu.SemaphoreType.DMA((10, chunks)),
            pltpu.SemaphoreType.DMA((10, chunks)),
            pltpu.SemaphoreType.DMA((2,)),
            pltpu.SemaphoreType.DMA,
            pltpu.SemaphoreType.DMA((2, 2)),
        ],
        compiler_params=pltpu.CompilerParams(
            collective_id=0, has_side_effects=True, vmem_limit_bytes=60 * 1024 * 1024
        ),
    )(
        query_rows,
        key_rows,
        value_rows,
        query_gain.reshape(hd, 1),
        key_gain.reshape(1, hd),
        selected,
        output_grad,
    )
    attended, query_grad, key_grad, value_grad, gains = outs
    return attended, query_grad, key_grad, value_grad, gains[0], gains[1]


def solution(mesh):
    rows = P("dp", "ctx", None)
    return jax.shard_map(
        functools.partial(local, dict(mesh.shape)),
        mesh=mesh,
        in_specs=(rows, rows, rows, P(), P(), rows, rows),
        out_specs=(rows, rows, rows, rows, P(), P()),
        check_vma=False,
    )
```

time: 727 us -> 339 us (0.47); the launches traced: 717 us -> 339 us
  Pallas kernels: 0 us -> 329 us
  waiting for transfers between devices: 215 us -> 0 us
  blocking collectives: 134 us -> 0 us
  local copies, waits for them, and re-layouts: 138 us -> 9.18 us
  matrix products: 94.3 us -> 0 us
  other arithmetic: 66.9 us -> 0 us
  starting transfers between devices: 65.5 us -> 0 us
    pallas_call x0 -> x1, Pallas kernels: none -> 329 us  [local(): pl.pallas_call(functools.partial(body, cfg), out_shape=(row, row, row, ro...]
    all_to_all x8 -> x0, waiting for transfers between devices: 215 us -> none  [the longest x1 71.2 us: local(): lax.all_to_all(remote_value_all, 'ctx', split_axis=2, concat_axis=0, tile...]
    dot_general x26 -> x0, matrix products: 94.3 us -> none  [the longest x4 20.9 us: attend(): jnp.einsum('qhd,khd->hqk', query_block, key_block, preferred_element_type...]
    psum x1 -> x0, blocking collectives: 85 us -> none  [local(): lax.psum((query_gain_part, key_gain_part), ('dp', 'ctx'))]
    all_to_all x8 -> x0, starting transfers between devices: 65.5 us -> none  [the longest x1 12.2 us: local(): lax.all_to_all(key_normed.reshape(local_count, block_size, model_width),...]
    all_gather x1 -> x0, blocking collectives: 48.7 us -> none  [local(): choice_table = lax.all_gather(selected[0], 'ctx', axis=0, tiled=True)]
    another operation x8 -> x0, local copies, waits for them, and re-layouts: 40 us -> none  [the longest x3 18.2 us: local(): jnp.stack([grad_term.astype(jnp.bfloat16) for grad_term in value_terms[1:]])]
    unnamed x88 -> x12, local copies, waits for them, and re-layouts: 44.6 us -> 7.18 us
  transfers between devices with their start and end apart: 8 -> 0, of which waited for: 5 -> 0; matrix products, arithmetic and copies ran while one was open for 23% -> 0% of each run, Pallas kernels for 0% -> 0%
where the time goes in v1:
time: 339 us
  Pallas kernels  329 us (97%)
  local copies, waits for them, and re-layouts  9.18 us (3%)
    pallas_call x1, Pallas kernels, local(): pl.pallas_call(functools.partial(body, cfg), out_shape=(row, row, row, ro...  329 us
    unnamed x12, local copies, waits for them, and re-layouts  7.18 us

profile of v1, /device:TPU:1, one launch (start us, length us, event | category | flops | bytes accessed | tf_op | source)
XLA Modules:
  0.0 339.0 jit_solution(8960805293184900366)
XLA Ops:
  0.6 0.0 copy-start.3
  0.6 0.6 copy-done.3
  1.3 0.7 copy.13.qg_ref
  2.0 329.2 %shard_map.118 = (bf16[1,512,1024]{2,1,0:T(8,128)(2,1)}, bf16[1,512,1024]{2,1,0:T(8,128)(2,1)}, bf16[1,512,1024]{2,1,0:T(8,128)(2,1)}, bf16[1,512,1024]{2,1,0:T(8,128)(2,1)}, f32[8,128]{1,0:T(8,128)}) custom-call(bf16[1,512,1024]{2,1,0:T(8,128)(2,1)} %q_ref.1, bf16[1,512,1024]{2,1,0:T(8,128)(2,1)} %k_ref.1, bf16[1,512,1024]{2,1,0:T(8,128)(2,1)} %v_ref.1, ...), custom_call_target="tpu_custom_call" | custom-call | tf_op jit(solution)/shard_map/pallas_call | solution.py:418
  331.2 1.3 slice_bitcast_fusion
  332.5 0.0 copy-start.2
  332.5 2.4 copy.18
  334.9 0.0 copy-done.2
  334.9 0.0 copy-start.1
  334.9 1.0 copy.19
  335.8 0.6 copy-done.1
  336.5 0.0 copy-start
  336.5 1.0 copy.20
  337.4 0.6 copy-done
  338.1 1.0 copy.21
Async XLA Ops:
  0.6 0.7 copy-start.3
  332.5 2.4 copy-start.2
  334.9 1.6 copy-start.1
  336.5 1.6 copy-start

commit v2 on v1

--- a/solution.py
+++ b/solution.py
@@ -7,7 +7,7 @@
 from jax.experimental.pallas import tpu as pltpu
 from jax.sharding import PartitionSpec as P
 
-CHUNKS = 2
+CHUNKS = 4
 EPS = 1e-06
 OWN, PREV, FIRST, MID = 0, 1, 2, 3
 F32, BF16 = jnp.float32, jnp.bfloat16
@@ -19,12 +19,12 @@
 
 def body(
     cfg,
-    q_ref, k_ref, v_ref, qg_ref, kg_ref, sel_ref, do_ref,
+    q_hbm, k_ref, v_ref, qg_ref, kg_ref, sel_ref, do_hbm,
     att_ref, dq_ref, dk_ref, dv_ref, gain_ref,
     kv, hold, pick, fetch, prev, first, w_scr,
     term, own_grad, back, part, sums, coll, prev_back, rx, rz_out, rz,
-    sel_tile, table, table_s, links, gq, gk, gbuf, gbuf2,
-    send_sem, recv_sem, sel_sem, local_sem, gain_sem,
+    sel_tile, table, links_v, links, gq, gk, gbuf, gbuf2,
+    send_sem, recv_sem, sel_sem, local_sem, gain_sem, q_ref, do_ref, in_sem,
 ):
     n, nx, nz, n_dp, chunks, heads, hd, block = (
         cfg[k] for k in ("n", "nx", "nz", "n_dp", "chunks", "heads", "hd", "block")
@@ -77,6 +77,10 @@
 
     HOLD, FETCH, BACK, COLL, PREV_F, PREV_B, AG_Z, AG_X, RS_X, RS_Z = range(10)
 
+    load_q = pltpu.make_async_copy(q_hbm, q_ref, in_sem.at[0])
+    load_do = pltpu.make_async_copy(do_hbm, do_ref, in_sem.at[1])
+    load_q.start()
+    load_do.start()
     barrier = pltpu.get_barrier_semaphore()
 
     def greet(peer):
@@ -106,8 +110,11 @@
 
         lax.fori_loop(0, per_chunk, step, 0)
 
+    gain_col = jnp.broadcast_to(qg_ref[...], (8, hd)).T[:, 0:1]
     norm_chunk(0)
-    sel_tile[...] = jnp.full(sel_tile.shape, sel_ref[0, 0, 1], jnp.int32)
+    sub = lax.broadcasted_iota(jnp.int32, (8, 128), 0)
+    lane = lax.broadcasted_iota(jnp.int32, (8, 128), 1)
+    sel_tile[...] = jnp.where((sub < 4) | (lane == me), sel_ref[0, 0, 1], 0)
     pl.semaphore_wait(barrier, n - 1 + n_dp - 1)
 
     def send_table(peer):
@@ -133,9 +140,6 @@
     send_hold(0)
     for c in range(1, chunks):
         norm_chunk(c)
-        send_hold(c)
-    for c in range(chunks):
-        send_prev(c)
 
     some = pltpu.make_async_remote_copy(
         src_ref=table.at[pl.ds(0, n - 1)],
@@ -146,26 +150,25 @@
         device_id_type=pl.DeviceIdType.MESH,
     )
     some.wait_recv()
-    to_scalars = pltpu.make_async_copy(table, table_s, local_sem)
+    choice = table[:, 0, :]
+    spread_out = table[0, 4:8, :]
+    for i in range(1, n):
+        spread_out = spread_out + table[i, 4:8, :]
+    across = jnp.broadcast_to(spread_out[0:1, :], (n, 128))
+    row_id = lax.broadcasted_iota(jnp.int32, (n, 128), 0)
+    lane_id = lax.broadcasted_iota(jnp.int32, (n, 128), 1)
+    before = jnp.where((across == choice) & (lane_id < row_id), lane_id, -1)
+    last = jnp.where((across == row_id) & (lane_id < n), lane_id, -1)
+    links_v[0] = choice
+    for k, found in ((1, before), (2, last)):
+        top = jnp.max(found, axis=-1, keepdims=True)
+        links_v[k] = jnp.broadcast_to(jnp.where(top < 0, n, top), (n, 128))
+    to_scalars = pltpu.make_async_copy(links_v, links, local_sem)
     to_scalars.start()
     to_scalars.wait()
 
-    def link(i, carry):
-        mine = table_s[i, 0, 0]
-
-        def look(o, found):
-            before, last = found
-            other = table_s[o, 0, 0]
-            before = jnp.where((o < i) & (other == mine), o, before)
-            last = jnp.where(other == i, o, last)
-            return before, last
-
-        before, last = lax.fori_loop(0, n, look, (jnp.int32(n), jnp.int32(n)))
-        links[0, i] = before
-        links[1, i] = last
-        return carry
-
-    lax.fori_loop(0, n, link, 0)
+    def link(kind, i):
+        return jnp.clip(links[kind, i, 0], 0, n if kind else n - 1)
 
     def serve(c):
         landed(hold[c].at[pl.ds(0, n - 1)], HOLD, c)
@@ -173,24 +176,31 @@
         each_z(lambda p, _: remote(first.at[c, me], first.at[c, me], AG_Z, c, p).start())
 
         def send(p):
-            pick[c, p] = hold[c][table_s[p, 0, 0]]
+            pick[c, p] = hold[c][link(0, p)]
             remote(pick.at[c, p], fetch.at[c, me], FETCH, c, p).start()
 
         each_peer(send)
-        fetch[c, me] = hold[c][table_s[me, 0, 0]]
+        fetch[c, me] = hold[c][link(0, me)]
 
     def spread(c):
         landed(first.at[c, pl.ds(0, nz - 1)], AG_Z, c)
         row = pl.ds(x * nz, nz)
         each_x(lambda p, _: remote(first.at[c, row], first.at[c, row], AG_X, c, p).start())
 
-    for c in range(chunks):
+    def prepare(c):
         serve(c)
+        if c + 1 < chunks:
+            send_hold(c + 1)
+        send_prev(c)
         spread(c)
+
+    prepare(0)
+    load_q.wait()
+    load_do.wait()
 
     see_prev = (me >= 2).astype(F32)
     see_first = (me >= 1).astype(F32)
-    see_mid = jnp.where(table_s[me, 0, 0] != me, 1.0, 0.0).astype(F32)
+    see_mid = jnp.where(links[0, me, 0] != me, 1.0, 0.0).astype(F32)
     see = (None, see_prev, see_first, see_mid)
     stores = (kv, prev, first, fetch)
 
@@ -206,7 +216,7 @@
             wide = pl.ds(pl.multiple_of(c * width + hh * hd, hd), hd)
             xt = q_ref[0, :, wide].astype(F32).T
             factor = lax.rsqrt(jnp.mean(xt * xt, axis=0, keepdims=True) + EPS)
-            gain = qg_ref[...]
+            gain = gain_col
             qn = (xt * factor * gain).astype(BF16)
             do = do_ref[0, :, wide].astype(F32).T
             do_b = do.astype(BF16)
@@ -266,7 +276,7 @@
         lax.fori_loop(0, per_chunk, step, 0)
 
     def give_back(c):
-        mid, head, before = term.at[MID - 1, c], term.at[FIRST - 1, c], term.at[PREV - 1, c]
+        mid, head = term.at[MID - 1, c], term.at[FIRST - 1, c]
         each_peer(lambda p: remote(mid.at[p], back.at[c, me], BACK, c, p).start())
         back[c, me] = term[MID - 1, c, me]
 
@@ -275,7 +285,11 @@
 
         each_x(send_row)
         rx[c, x] = term[FIRST - 1, c, pl.ds(x * nz, nz)]
-        remote(before, prev_back.at[c], PREV_B, c, down).start()
+        if c + 1 < chunks:
+            send_prev_back(c)
+
+    def send_prev_back(c):
+        remote(term.at[PREV - 1, c], prev_back.at[c], PREV_B, c, down).start()
 
     def fold_first(c):
         landed(rx.at[c, pl.ds(0, nx - 1)], RS_X, c)
@@ -293,21 +307,23 @@
 
     def collect(c):
         landed(back.at[c, pl.ds(0, n - 1)], BACK, c)
+        if c + 1 == chunks:
+            send_prev_back(c)
         part[n] = jnp.zeros(part.shape[1:], F32)
 
         def add(i, carry):
-            part[i] = back[c, i].astype(F32) + part[links[0, i]]
+            part[i] = back[c, i].astype(F32) + part[link(1, i)]
             return carry
 
         lax.fori_loop(0, n, add, 0)
 
         def settle(j, carry):
-            sums[c, j] = part[links[1, j]].astype(BF16)
+            sums[c, j] = part[link(2, j)].astype(BF16)
             return carry
 
         lax.fori_loop(1, n, settle, 0)
         landed(rz.at[c, pl.ds(0, nz - 1)], RS_Z, c)
-        total = part[links[1, 0]]
+        total = part[link(2, 0)]
         for k in range(nz):
             total = total + rz[c, k].astype(F32)
         sums[c, 0] = total.astype(BF16)
@@ -341,6 +357,8 @@
         lax.fori_loop(0, per_chunk, step, 0)
 
     for c in range(chunks):
+        if c + 1 < chunks:
+            prepare(c + 1)
         landed(prev.at[c], PREV_F, c)
         landed(fetch.at[c, pl.ds(0, n - 1)], FETCH, c)
         landed(first.at[c, pl.ds(0, (nx - 1) * nz)], AG_X, c)
@@ -415,10 +433,11 @@
     vmem = pltpu.VMEM
     row = jax.ShapeDtypeStruct((1, block, model), BF16)
     whole = pl.BlockSpec(memory_space=pltpu.VMEM)
+    anywhere = pl.BlockSpec(memory_space=pl.ANY)
     outs = pl.pallas_call(
         functools.partial(body, cfg),
         out_shape=(row, row, row, row, jax.ShapeDtypeStruct((8, hd), F32)),
-        in_specs=[whole] * 5 + [pl.BlockSpec(memory_space=pltpu.SMEM), whole],
+        in_specs=[anywhere] + [whole] * 4 + [pl.BlockSpec(memory_space=pltpu.SMEM), anywhere],
         out_specs=(whole,) * 5,
         scratch_shapes=[
             vmem(slices, BF16),
@@ -440,8 +459,8 @@
             vmem((chunks, nz, 2 * rows, width), BF16),
             vmem((8, 128), jnp.int32),
             vmem((n, 8, 128), jnp.int32),
-            pltpu.SMEM((n, 8, 128), jnp.int32),
-            pltpu.SMEM((2, n), jnp.int32),
+            vmem((3, n, 128), jnp.int32),
+            pltpu.SMEM((3, n, 128), jnp.int32),
             vmem((hd, hd), F32),
             vmem((8, hd), F32),
             vmem((n, 8, hd), F32),
@@ -451,6 +470,9 @@
             pltpu.SemaphoreType.DMA((2,)),
             pltpu.SemaphoreType.DMA,
             pltpu.SemaphoreType.DMA((2, 2)),
+            vmem((1, block, model), BF16),
+            vmem((1, block, model), BF16),
+            pltpu.SemaphoreType.DMA((2,)),
         ],
         compiler_params=pltpu.CompilerParams(
             collective_id=0, has_side_effects=True, vmem_limit_bytes=60 * 1024 * 1024
@@ -459,7 +481,7 @@
         query_rows,
         key_rows,
         value_rows,
-        query_gain.reshape(hd, 1),
+        query_gain.reshape(1, hd),
         key_gain.reshape(1, hd),
         selected,
         output_grad,

time: 339 us -> 308 us (0.909)
  Pallas kernels: 329 us -> 299 us
    pallas_call x1, Pallas kernels: 329 us -> 299 us  [local(): pl.pallas_call(functools.partial(body, cfg), out_shape=(row, row, row, ro...]
    unnamed x12 -> x10, local copies, waits for them, and re-layouts: 7.18 us -> 6.53 us
where the time goes in v2:
time: 308 us
  Pallas kernels  299 us (97%)
  local copies, waits for them, and re-layouts  7.8 us (3%)
    pallas_call x1, Pallas kernels, local(): pl.pallas_call(functools.partial(body, cfg), out_shape=(row, row, row, ro...  299 us
    unnamed x10, local copies, waits for them, and re-layouts  6.53 us

profile of v2, /device:TPU:1, one launch (start us, length us, event | category | flops | bytes accessed | tf_op | source)
XLA Modules:
  0.0 307.9 jit_solution(13772912371957266275)
XLA Ops:
  0.6 299.5 %shard_map.118 = (bf16[1,512,1024]{2,1,0:T(8,128)(2,1)}, bf16[1,512,1024]{2,1,0:T(8,128)(2,1)}, bf16[1,512,1024]{2,1,0:T(8,128)(2,1)}, bf16[1,512,1024]{2,1,0:T(8,128)(2,1)}, f32[8,128]{1,0:T(8,128)}) custom-call(bf16[1,512,1024]{2,1,0:T(8,128)(2,1)} %q_hbm.1, bf16[1,512,1024]{2,1,0:T(8,128)(2,1)} %k_ref.1, bf16[1,512,1024]{2,1,0:T(8,128)(2,1)} %v_ref.1, ...), custom_call_target="tpu_custom_call" | custom-call | tf_op jit(solution)/shard_map/pallas_call | solution.py:437
  300.1 1.3 slice_bitcast_fusion
  301.4 0.0 copy-start.2
  301.4 2.4 copy.17
  303.7 0.0 copy-done.2
  303.7 0.0 copy-start.1
  303.7 1.0 copy.18
  304.7 0.6 copy-done.1
  305.3 0.0 copy-start
  305.3 1.0 copy.19
  306.3 0.6 copy-done
  306.9 1.0 copy.20
Async XLA Ops:
  301.4 2.4 copy-start.2
  303.7 1.6 copy-start.1
  305.3 1.6 copy-start

commit v3 on v2

--- a/solution.py
+++ b/solution.py
@@ -20,7 +20,7 @@
 def body(
     cfg,
     q_hbm, k_ref, v_ref, qg_ref, kg_ref, sel_ref, do_hbm,
-    att_ref, dq_ref, dk_ref, dv_ref, gain_ref,
+    att_ref, dq_ref, dk_ref, dv_ref, q_gain_ref, k_gain_ref,
     kv, hold, pick, fetch, prev, first, w_scr,
     term, own_grad, back, part, sums, coll, prev_back, rx, rz_out, rz,
     sel_tile, table, links_v, links, gq, gk, gbuf, gbuf2,
@@ -410,13 +410,19 @@
     total = gbuf2[0]
     for i in range(1, n_dp):
         total = total + gbuf2[i]
-    gain_ref[...] = total
+    q_gain_ref[...] = total[0:1, :]
+    k_gain_ref[...] = total[1:2, :]
 
     all_gain(gbuf, n, 0).wait_send()
     all_gain(gbuf2, n_dp, 1).wait_send()
     some.wait_send()
     for like, stage, c in waits:
         remote(like, like, stage, c, up).wait_send()
+
+
+def hand_over(*refs):
+    for given, taken in zip(refs[0:6], refs[6:12], strict=True):
+        taken[...] = given[...]
 
 
 def local(mesh_shape, query_rows, key_rows, value_rows, query_gain, key_gain, selected, output_grad):
@@ -432,13 +438,14 @@
     slices = (chunks, n, 2 * rows, width)
     vmem = pltpu.VMEM
     row = jax.ShapeDtypeStruct((1, block, model), BF16)
+    gain = jax.ShapeDtypeStruct((1, hd), F32)
     whole = pl.BlockSpec(memory_space=pltpu.VMEM)
     anywhere = pl.BlockSpec(memory_space=pl.ANY)
     outs = pl.pallas_call(
         functools.partial(body, cfg),
-        out_shape=(row, row, row, row, jax.ShapeDtypeStruct((8, hd), F32)),
+        out_shape=(row, row, row, row, gain, gain),
         in_specs=[anywhere] + [whole] * 4 + [pl.BlockSpec(memory_space=pltpu.SMEM), anywhere],
-        out_specs=(whole,) * 5,
+        out_specs=(whole,) * 6,
         scratch_shapes=[
             vmem(slices, BF16),
             [vmem(slices[1:], BF16)] * chunks,
@@ -486,8 +493,18 @@
         selected,
         output_grad,
     )
-    attended, query_grad, key_grad, value_grad, gains = outs
-    return attended, query_grad, key_grad, value_grad, gains[0], gains[1]
+    steps = 4
+    part = pl.BlockSpec((1, block // steps, model), lambda i: (0, i, 0))
+    line = pl.BlockSpec((1, hd), lambda i: (0, 0))
+    outs = pl.pallas_call(
+        hand_over,
+        out_shape=(row, row, row, row, gain, gain),
+        grid=(steps,),
+        in_specs=[part] * 4 + [line] * 2,
+        out_specs=(part,) * 4 + (line,) * 2,
+    )(*outs)
+    attended, query_grad, key_grad, value_grad, q_gain, k_gain = outs
+    return attended, query_grad, key_grad, value_grad, q_gain.reshape(hd), k_gain.reshape(hd)
 
 
 def solution(mesh):

time: 308 us -> 305 us (level)
  local copies, waits for them, and re-layouts: 7.8 us -> 0 us
  Pallas kernels: 299 us -> 304 us
    unnamed x10 -> x0, local copies, waits for them, and re-layouts: 6.53 us -> none
    pallas_call x0 -> x1, Pallas kernels: none -> 4.67 us  [local(): pl.pallas_call(hand_over, out_shape=(row, row, row, row, gain, gain), gri...]
where the time goes in v3:
time: 305 us; the launch traced here: 304 us
  Pallas kernels  304 us (100%)
    pallas_call x1, Pallas kernels, local(): pl.pallas_call(functools.partial(body, cfg), out_shape=(row, row, row, ro...  299 us

profile of v3, /device:TPU:1, one launch (start us, length us, event | category | flops | bytes accessed | tf_op | source)
XLA Modules:
  0.0 304.5 jit_solution(949061293587373206)
XLA Ops:
  0.6 299.0 %shard_map.118 = (bf16[1,512,1024]{2,1,0:T(8,128)(2,1)}, bf16[1,512,1024]{2,1,0:T(8,128)(2,1)}, bf16[1,512,1024]{2,1,0:T(8,128)(2,1)}, bf16[1,512,1024]{2,1,0:T(...) custom-call(bf16[1,512,1024]{2,1,0:T(8,128)(2,1)} %q_hbm.1, bf16[1,512,1024]{2,1,0:T(8,128)(2,1)} %k_ref.1, ...), custom_call_target="tpu_custom_call" | custom-call | tf_op jit(solution)/shard_map/pallas_call | solution.py:444
  299.7 4.7 %shard_map.119 = (bf16[1,512,1024]{2,1,0:T(8,128)(2,1)}, bf16[1,512,1024]{2,1,0:T(8,128)(2,1)}, bf16[1,512,1024]{2,1,0:T(8,128)(2,1)}, bf16[1,512,1024]{2,1,0:T(...) custom-call(bf16[1,512,1024]{2,1,0:T(8,128)(2,1)} %get-tuple-element.18.refs_0_, ...), custom_call_target="tpu_custom_call" | custom-call | tf_op jit(solution)/shard_map/pallas_call | solution.py:499

commit v4 on v3

--- a/solution.py
+++ b/solution.py
@@ -322,12 +322,23 @@
             return carry
 
         lax.fori_loop(1, n, settle, 0)
+
+        def settled(p):
+            @pl.when(p != 0)
+            def _():
+                remote(sums.at[c, p], coll.at[c, me], COLL, c, p).start()
+
+        each_peer(settled)
         landed(rz.at[c, pl.ds(0, nz - 1)], RS_Z, c)
         total = part[link(2, 0)]
         for k in range(nz):
             total = total + rz[c, k].astype(F32)
         sums[c, 0] = total.astype(BF16)
-        each_peer(lambda p: remote(sums.at[c, p], coll.at[c, me], COLL, c, p).start())
+
+        @pl.when(me != 0)
+        def _():
+            remote(sums.at[c, 0], coll.at[c, me], COLL, c, 0).start()
+
         coll[c, me] = sums[c, me]
 
     def finish(c):

time: 305 us -> 300 us (0.984)
  Pallas kernels: 304 us -> 299 us
    pallas_call x1, Pallas kernels: 299 us -> 294 us  [local(): pl.pallas_call(functools.partial(body, cfg), out_shape=(row, row, row, ro...]
where the time goes in v4:
time: 300 us
  Pallas kernels  299 us (100%)
    pallas_call x1, Pallas kernels, local(): pl.pallas_call(functools.partial(body, cfg), out_shape=(row, row, row, ro...  294 us

profile of v4, /device:TPU:1, one launch (start us, length us, event | category | flops | bytes accessed | tf_op | source)
XLA Modules:
  0.0 299.6 jit_solution(15528714986929493485)
XLA Ops:
  0.6 294.1 %shard_map.118 = (bf16[1,512,1024]{2,1,0:T(8,128)(2,1)}, bf16[1,512,1024]{2,1,0:T(8,128)(2,1)}, bf16[1,512,1024]{2,1,0:T(8,128)(2,1)}, bf16[1,512,1024]{2,1,0:T(...) custom-call(bf16[1,512,1024]{2,1,0:T(8,128)(2,1)} %q_hbm.1, bf16[1,512,1024]{2,1,0:T(8,128)(2,1)} %k_ref.1, ...), custom_call_target="tpu_custom_call" | custom-call | tf_op jit(solution)/shard_map/pallas_call | solution.py:455
  294.8 4.7 %shard_map.119 = (bf16[1,512,1024]{2,1,0:T(8,128)(2,1)}, bf16[1,512,1024]{2,1,0:T(8,128)(2,1)}, bf16[1,512,1024]{2,1,0:T(8,128)(2,1)}, bf16[1,512,1024]{2,1,0:T(...) custom-call(bf16[1,512,1024]{2,1,0:T(8,128)(2,1)} %get-tuple-element.18.refs_0_, ...), custom_call_target="tpu_custom_call" | custom-call | tf_op jit(solution)/shard_map/pallas_call | solution.py:510
